TPU v7x, 256 devices: a whole 4x4x8 slice. The times are simulated.
256 devices in a mesh: cells: 64 (over x, z, core), rhs: 4 (over y).
Axes of the slice: x: 4, y: 4, z: 8, core: 2. Of those that a mesh axis runs over, the one named last changes fastest.
Arguments:
- right_side: bfloat16 [512, 512, 384], P('cells', 'rhs'), may hold values from -6 to 6
- leaf_inverse: bfloat16 [512, 384, 384], P('cells'), may hold values from -0.3125 to 0.3125
- leaf_couple: bfloat16 [512, 9, 384, 128], P('cells'), may hold values from -0.3125 to 0.3125
- skel_target: int32 [512, 9], P('cells'), may hold values from 0 to 2047, as said below
- skeleton_in: float32 [512, 2048, 128], P('rhs', 'cells'), may hold values from -6 to 6
- lift_ops: bfloat16 [64, 4096, 512], P('cells', None, 'rhs'), may hold values from -0.09375 to 0.09375
- node_mix: bfloat16 [64, 1024, 512], P('cells', None, 'rhs'), may hold values from -0.1875 to 0.1875
- node_couple: bfloat16 [64, 512, 512], P('cells', None, 'rhs'), may hold values from -0.125 to 0.125
Outputs:
- leaf_solution: bfloat16 [512, 512, 384], P('cells', 'rhs')
- skeleton_rhs: float32 [512, 2048, 128], P('rhs', 'cells')
- node_solution: bfloat16 [64, 512, 512], P('cells', 'rhs')
- node_skeleton: float32 [64, 512, 512], P('cells', 'rhs')
Inputs may be any that keep to these rules, and one draw needn't show every extreme that they name: `skel_target`: entry (c, k) names a skeleton block; its owner device, the entry // 32, lies at most 2 positions along cells from the cell's device c // 8, and on every device some slot reaches that distance.
All inputs are finite; a program needn't handle non-finite values.
Results may differ from a plain program's by a relative error of at most 0.03.
Values may be sent and summed in bfloat16 or wider, within the bound.
No kernel may reach another device: no remote copies, remote signals or barrier semaphores. Data moves between devices by JAX's collectives and lax.ppermute only.
A program may use at most 128 MiB of HBM per device.

v0:
```python
import jax
import jax.numpy as jnp
from jax import lax
from jax.sharding import PartitionSpec as P

HOP = 2


def passed_along(value, axis, steps):
    count = lax.axis_size(axis)
    initial, last = (max(0, -steps), min(count, count - steps))
    return lax.ppermute(value, axis, [(source, source + steps) for source in range(initial, last)])


def passed_along_2(value, axis, by):
    devices = lax.axis_size(axis)
    return lax.ppermute(value, axis, [(i, (i + by) % devices) for i in range(devices)])


def on_device(
    right_side, leaf_inverse, leaf_couple, skel_target, skeleton_in, lift_ops, node_mix, node_couple
):
    position = lax.axis_index("cells")
    total_devices = lax.axis_size("cells")
    levels = total_devices.bit_length() - 1
    columns = right_side.shape[1]
    blocks = skeleton_in.shape[1]
    block_width = skeleton_in.shape[2]
    solved = jnp.einsum(
        "ncr,nrq->ncq", right_side, leaf_inverse, preferred_element_type=jnp.float32
    ).astype(jnp.bfloat16)
    updates = jnp.einsum("ncr,nkrs->nkcs", solved, leaf_couple, preferred_element_type=jnp.float32)
    slot_count = updates.shape[0] * updates.shape[1]
    updates = updates.reshape(slot_count, columns, block_width)
    targets = skel_target.reshape(slot_count)
    owners = targets // blocks
    within = targets % blocks
    offsets = owners - position
    hop_reach = HOP
    span_rows = 2 * hop_reach + 1
    segment_ids = (offsets + hop_reach) * blocks + within
    summed = jax.ops.segment_sum(updates, segment_ids, num_segments=span_rows * blocks)
    portions = jnp.transpose(summed.reshape(span_rows, blocks, columns, block_width), (0, 2, 1, 3))
    arrived = portions[hop_reach]
    for distance in list(range(-hop_reach, 0)) + list(range(1, hop_reach + 1)):
        arrived = arrived + passed_along(
            portions[hop_reach + distance].astype(jnp.bfloat16), "cells", distance
        ).astype(jnp.float32)
    skeleton_rhs = skeleton_in - arrived
    gathered = (
        lax.all_gather(lift_ops[0], "rhs", axis=1, tiled=True),
        lax.all_gather(node_mix[0], "rhs", axis=1, tiled=True),
        lax.all_gather(node_couple[0], "rhs", axis=1, tiled=True),
    )

    def multiply(operand, which_op):
        return jnp.dot(operand, gathered[which_op], preferred_element_type=jnp.float32)

    def merge_node(left_child, right_child):
        joined = jnp.concatenate([left_child, right_child], axis=1)
        solution = multiply(joined, 1).astype(jnp.bfloat16)
        skeleton = 0.5 * (
            left_child.astype(jnp.float32) + right_child.astype(jnp.float32)
        ) - multiply(solution, 2)
        return (solution, skeleton)

    flattened = skeleton_rhs.reshape(columns, blocks * block_width).astype(jnp.bfloat16)
    current = multiply(flattened, 0).astype(jnp.bfloat16)
    level_solution = jnp.zeros_like(current)
    for section_level in range(1, levels + 1):
        distance = max(1, 2 ** (section_level - 2))
        left_child = passed_along_2(current, "cells", distance)
        if section_level == 1:
            right_child = current
        else:
            right_child = passed_along_2(current, "cells", -distance)
        level_solution, skeleton = merge_node(left_child, right_child)
        current = skeleton.astype(jnp.bfloat16)
    root_pair = passed_along_2(jnp.stack([current, level_solution]), "cells", -(total_devices // 2))
    node_solution, node_skeleton = merge_node(root_pair[0], root_pair[1])
    return (solved, skeleton_rhs, node_solution[None], node_skeleton[None])


def solution(mesh):
    return jax.shard_map(
        on_device,
        mesh=mesh,
        in_specs=(
            P("cells", "rhs", None),
            P("cells", None, None),
            P("cells", None, None, None),
            P("cells", None),
            P("rhs", "cells", None),
            P("cells", None, "rhs"),
            P("cells", None, "rhs"),
            P("cells", None, "rhs"),
        ),
        out_specs=(
            P("cells", "rhs", None),
            P("rhs", "cells", None),
            P("cells", "rhs", None),
            P("cells", "rhs", None),
        ),
        check_vma=False,
    )
```

profile of v0, /device:TPU:6, one launch (start us, length us, event | category | flops | bytes accessed | tf_op | source)
XLA Modules:
  0.0 207.8 jit_solution(803400362444438331)
XLA Ops:
  10.7 7.0 %fusion.27 = f32[8,128,9,128]{3,1,2,0:T(8,128)} fusion(bf16[8,9,384,128]{3,2,1,0:T(8,128)(2,1)} %param.10, bf16[8,128,384]{2,1,0:T(8,128)(2,1)S(1)} %convolution_convert_fusion), kind=kOutput, calls=%fused_computation.34 | convolution fusion | flops 905969664 | bytes 12582912 | tf_op jit(solution)/shard_map/ncr,nkrs->nkcs/dot_general | solution.py:32
  17.7 5.2 %broadcast_in_dim.10 = f32[160,128,128]{2,1,0:T(8,128)} broadcast(f32[]{:T(128)} %constant.30.clone.1), dimensions={} | broadcast | bytes 10485764 | tf_op jit(solution)/shard_map/broadcast_in_dim | solution.py:42
  22.9 17.1 %scatter_fusion = f32[160,128,128]{2,1,0:T(8,128)} fusion(f32[160,128,128]{2,1,0:T(8,128)} %broadcast_in_dim.10, s32[72]{0:T(128)S(1)} %fusion.76, f32[72,128,128]{2,1,0:T(8,128)} %bitcast.121), kind=kCustom, calls=%fused_computation | custom fusion | flops 1179648 | bytes 14156064 | tf_op jit(solution)/shard_map/scatter-add | solution.py:42
  40.0 5.4 %convert.6 = bf16[5,128,32,128]{3,1,2,0:T(8,128)(2,1)S(1)} convert(f32[5,128,32,128]{3,1,2,0:T(8,128)} %bitcast.119) | non-fusion elementwise | flops 2621440 | bytes 15728640 | tf_op jit(solution)/shard_map/convert.3
  47.5 8.0 %collective-permute-start = (bf16[128,32,128]{2,0,1:T(8,128)(2,1)}, bf16[128,32,128]{2,0,1:T(8,128)(2,1)S(1)}, u32[]{:S(2)}, u32[]{:S(2)}) collective-permute-start(bf16[128,32,128]{2,0,1:T(8,128)(2,1)} %get-tuple-element.14), channel_id=1, source_target_pairs={{8,0},{12,4},{16,8},{20,12},{24,16},{28,20},{32,24},{36,28},{40,32... | collective-permute-start | bytes 3145736 | tf_op jit(solution)/shard_map/ppermute | solution.py:12
  62.4 15.7 %collective-permute-done = bf16[128,32,128]{2,0,1:T(8,128)(2,1)S(1)} collective-permute-done((bf16[128,32,128]{2,0,1:T(8,128)(2,1)}, bf16[128,32,128]{2,0,1:T(8,128)(2,1)S(1)}, u32[]{:S(2)}, u32[]{:S(2)}) %collective-permute-start) | collective-permute-done | bytes 1048608 | tf_op jit(solution)/shard_map/ppermute | solution.py:12
  78.1 11.2 %collective-permute-done.1 = bf16[128,32,128]{2,0,1:T(8,128)(2,1)} collective-permute-done((bf16[128,32,128]{2,0,1:T(8,128)(2,1)}, bf16[128,32,128]{2,0,1:T(8,128)(2,1)}, u32[]{:S(2)}, u32[]{:S(2)}) %collective-permute-start.1) | collective-permute-done | bytes 1048608 | tf_op jit(solution)/shard_map/ppermute | solution.py:12
  90.3 6.6 %fusion.119 = (bf16[128,32,128]{2,0,1:T(8,128)(2,1)}, f32[128,32,128]{2,0,1:T(8,128)}) fusion(bf16[128,32,128]{2,0,1:T(8,128)(2,1)} %collective-permute-done.3, bf16[128,32,128]{2,0,1:T(8,128)(2,1)} %collective-permute-done.2, bf16[128,32,128]{2,0,1:T(8,128)(2,1)} %collective-permute-done.1, bf16[128,32,128]{2,0,1:T(8,128)(2,1)S(1)} %collective-permute-done, ...), kind=kLoop, calls=%fused_computation.91 | loop fusion | flops 5242880 | bytes 11534336 | tf_op jit(solution)/shard_map/convert_element_type | solution.py:67
  98.5 2.9 %fusion.7 = bf16[128,512]{1,0:T(8,128)(2,1)S(1)} fusion(bf16[128,4096]{0,1:T(8,128)(2,1)S(1)} %bitcast.122, bf16[1,4096,512]{2,1,0:T(8,128)(2,1)} %all-gather.6.cloned.1.call-done), kind=kOutput, calls=%fused_computation.10 | convolution fusion | flops 536936448 | bytes 5373952 | tf_op jit(solution)/shard_map/dot_general | solution.py:57
  101.5 8.1 %collective-permute-start.4 = (bf16[128,512]{1,0:T(8,128)(2,1)S(1)}, bf16[128,512]{1,0:T(8,128)(2,1)}, u32[]{:S(2)}, u32[]{:S(2)}) collective-permute-start(bf16[128,512]{1,0:T(8,128)(2,1)S(1)} %fusion.7), channel_id=1, source_target_pairs={{0,4},{4,8},{8,12},{12,16},{16,20},{20,24},{24,28},{28,32},{32,36}... | collective-permute-start | bytes 393224 | tf_op jit(solution)/shard_map/ppermute | solution.py:17
  109.5 15.8 %all-gather.2 = bf16[1,512,512]{2,1,0:T(8,128)(2,1)} all-gather(bf16[1,512,128]{2,1,0:T(8,128)(2,1)} %param.15), channel_id=4, replica_groups=mesh['cells'=64,'rhs'=4] {'rhs'}, dimensions={2}, use_global_device_ids=true | all-gather | bytes 655360 | tf_op jit(solution)/shard_map/all_gather | solution.py:53
  125.4 2.6 %subtract_convert_fusion.5 = bf16[128,512]{1,0:T(8,128)(2,1)} fusion(bf16[128,512]{1,0:T(8,128)(2,1)S(1)} %fusion.7, bf16[128,512]{1,0:T(8,128)(2,1)} %collective-permute-done.4, bf16[1,512,512]{2,1,0:T(8,128)(2,1)} %all-gather.2, bf16[1,1024,512]{2,1,0:T(8,128)(2,1)} %all-gather.8.cloned.1.call-done), kind=kOutput, calls=%fused_computation.73 | convolution fusion | flops 202309632 | bytes 1966080 | tf_op jit(solution)/shard_map/dot_general | solution.py:57
  128.0 3.9 %collective-permute-start.6 = (bf16[128,512]{1,0:T(8,128)(2,1)}, bf16[128,512]{1,0:T(8,128)(2,1)}, u32[]{:S(2)}, u32[]{:S(2)}) collective-permute-start(bf16[128,512]{1,0:T(8,128)(2,1)} %subtract_convert_fusion.5), channel_id=1, source_target_pairs={{0,252},{4,0},{8,4},{12,8},{16,12},{20,16},{24,20},{28,24},{32,28}... | collective-permute-start | bytes 393224 | tf_op jit(solution)/shard_map/ppermute | solution.py:17
  131.9 2.9 %collective-permute-done.5 = bf16[128,512]{1,0:T(8,128)(2,1)S(1)} collective-permute-done((bf16[128,512]{1,0:T(8,128)(2,1)}, bf16[128,512]{1,0:T(8,128)(2,1)S(1)}, u32[]{:S(2)}, u32[]{:S(2)}) %collective-permute-start.5) | collective-permute-done | bytes 131104 | tf_op jit(solution)/shard_map/ppermute | solution.py:17
  134.7 2.6 %subtract_convert_fusion.4 = bf16[128,512]{1,0:T(8,128)(2,1)} fusion(bf16[128,512]{1,0:T(8,128)(2,1)} %collective-permute-done.6, bf16[128,512]{1,0:T(8,128)(2,1)S(1)} %collective-permute-done.5, bf16[1,512,512]{2,1,0:T(8,128)(2,1)} %all-gather.2, bf16[1,1024,512]{2,1,0:T(8,128)(2,1)} %all-gather.8.cloned.1.call-done), kind=kOutput, calls=%fused_computation.72 | convolution fusion | flops 202309632 | bytes 1966080 | tf_op jit(solution)/shard_map/dot_general | solution.py:57
  137.3 4.1 %collective-permute-start.8 = (bf16[128,512]{1,0:T(8,128)(2,1)}, bf16[128,512]{1,0:T(8,128)(2,1)}, u32[]{:S(2)}, u32[]{:S(2)}) collective-permute-start(bf16[128,512]{1,0:T(8,128)(2,1)} %subtract_convert_fusion.4), channel_id=1, source_target_pairs={{0,248},{4,252},{8,0},{12,4},{16,8},{20,12},{24,16},{28,20},{32,24... | collective-permute-start | bytes 393224 | tf_op jit(solution)/shard_map/ppermute | solution.py:17
  141.4 4.1 %collective-permute-done.7 = bf16[128,512]{1,0:T(8,128)(2,1)S(1)} collective-permute-done((bf16[128,512]{1,0:T(8,128)(2,1)}, bf16[128,512]{1,0:T(8,128)(2,1)S(1)}, u32[]{:S(2)}, u32[]{:S(2)}) %collective-permute-start.7) | collective-permute-done | bytes 131104 | tf_op jit(solution)/shard_map/ppermute | solution.py:17
  150.7 4.2 %collective-permute-done.10 = bf16[128,512]{1,0:T(8,128)(2,1)S(1)} collective-permute-done((bf16[128,512]{1,0:T(8,128)(2,1)}, bf16[128,512]{1,0:T(8,128)(2,1)S(1)}, u32[]{:S(2)}, u32[]{:S(2)}) %collective-permute-start.10) | collective-permute-done | bytes 131104 | tf_op jit(solution)/shard_map/ppermute | solution.py:17
  154.9 5.9 %collective-permute-done.9 = bf16[128,512]{1,0:T(8,128)(2,1)} collective-permute-done((bf16[128,512]{1,0:T(8,128)(2,1)}, bf16[128,512]{1,0:T(8,128)(2,1)}, u32[]{:S(2)}, u32[]{:S(2)}) %collective-permute-start.9) | collective-permute-done | bytes 131104 | tf_op jit(solution)/shard_map/ppermute | solution.py:17
  163.0 6.8 %collective-permute-start.12 = (bf16[128,512]{1,0:T(8,128)(2,1)}, bf16[128,512]{1,0:T(8,128)(2,1)}, u32[]{:S(2)}, u32[]{:S(2)}) collective-permute-start(bf16[128,512]{1,0:T(8,128)(2,1)} %subtract_convert_fusion.2), channel_id=1, source_target_pairs={{0,224},{4,228},{8,232},{12,236},{16,240},{20,244},{24,248},{28,25... | collective-permute-start | bytes 393224 | tf_op jit(solution)/shard_map/ppermute | solution.py:17
  169.8 9.0 %collective-permute-done.11 = bf16[128,512]{1,0:T(8,128)(2,1)S(1)} collective-permute-done((bf16[128,512]{1,0:T(8,128)(2,1)}, bf16[128,512]{1,0:T(8,128)(2,1)S(1)}, u32[]{:S(2)}, u32[]{:S(2)}) %collective-permute-start.11) | collective-permute-done | bytes 131104 | tf_op jit(solution)/shard_map/ppermute | solution.py:17
  183.2 3.2 %collective-permute-done.13 = bf16[128,512]{1,0:T(8,128)(2,1)S(1)} collective-permute-done((bf16[128,512]{1,0:T(8,128)(2,1)}, bf16[128,512]{1,0:T(8,128)(2,1)S(1)}, u32[]{:S(2)}, u32[]{:S(2)}) %collective-permute-start.13) | collective-permute-done | bytes 131104 | tf_op jit(solution)/shard_map/ppermute | solution.py:17
  186.4 2.9 %collective-permute-done.14 = bf16[128,512]{1,0:T(8,128)(2,1)S(1)} collective-permute-done((bf16[128,512]{1,0:T(8,128)(2,1)}, bf16[128,512]{1,0:T(8,128)(2,1)S(1)}, u32[]{:S(2)}, u32[]{:S(2)}) %collective-permute-start.14) | collective-permute-done | bytes 131104 | tf_op jit(solution)/shard_map/ppermute | solution.py:17
  194.8 4.8 %collective-permute-done.15 = bf16[2,128,512]{2,1,0:T(8,128)(2,1)S(1)} collective-permute-done((bf16[2,128,512]{2,1,0:T(8,128)(2,1)S(1)}, bf16[2,128,512]{2,1,0:T(8,128)(2,1)S(1)}, u32[]{:S(2)}, u32[]{:S(2)}) %collective-permute-start.15) | collective-permute-done | bytes 262176 | tf_op jit(solution)/shard_map/ppermute | solution.py:17
  (50 shorter events, 33.5 us)
Async XLA Ops:
  7.2 1.7 copy-start
  7.2 91.3 %all-gather.6.cloned.1.call-start = ((), (), s32[]{:S(2)}) async-start(), calls=%async_computation | async-start | bytes 5242880 | tf_op jit(solution)/shard_map/all_gather | solution.py:51
  7.9 117.5 %all-gather.8.cloned.1.call-start = ((), (), s32[]{:S(2)}) async-start(), calls=%async_computation.1 | async-start | bytes 1310720 | tf_op jit(solution)/shard_map/all_gather | solution.py:52
  10.7 7.0 %copy-start.4 = (bf16[8,128,384]{2,1,0:T(8,128)(2,1)}, bf16[8,128,384]{2,1,0:T(8,128)(2,1)S(1)}, u32[]{:S(2)}) copy-start(bf16[8,128,384]{2,1,0:T(8,128)(2,1)S(1)} %convolution_convert_fusion) | copy-start | bytes 2359300
  47.5 30.6 %collective-permute-start = (bf16[128,32,128]{2,0,1:T(8,128)(2,1)}, bf16[128,32,128]{2,0,1:T(8,128)(2,1)S(1)}, u32[]{:S(2)}, u32[]{:S(2)}) collective-permute-start(bf16[128,32,128]{2,0,1:T(8,128)(2,1)} %get-tuple-element.14), channel_id=1, source_target_pairs={{8,0},{12,4},{16,8},{20,12},{24,16},{28,20},{32,24},{36,28},{40,32... | collective-permute-start | bytes 3145736 | tf_op jit(solution)/shard_map/ppermute | solution.py:12
  55.5 33.8 %collective-permute-start.1 = (bf16[128,32,128]{2,0,1:T(8,128)(2,1)}, bf16[128,32,128]{2,0,1:T(8,128)(2,1)}, u32[]{:S(2)}, u32[]{:S(2)}) collective-permute-start(bf16[128,32,128]{2,0,1:T(8,128)(2,1)} %get-tuple-element.17), channel_id=1, source_target_pairs={{4,0},{8,4},{12,8},{16,12},{20,16},{24,20},{28,24},{32,28},{36,32}... | collective-permute-start | bytes 3145736 | tf_op jit(solution)/shard_map/ppermute | solution.py:12
  57.5 31.9 %collective-permute-start.2 = (bf16[128,32,128]{2,0,1:T(8,128)(2,1)}, bf16[128,32,128]{2,0,1:T(8,128)(2,1)}, u32[]{:S(2)}, u32[]{:S(2)}) collective-permute-start(bf16[128,32,128]{2,0,1:T(8,128)(2,1)} %get-tuple-element.16), channel_id=1, source_target_pairs={{0,4},{4,8},{8,12},{12,16},{16,20},{20,24},{24,28},{28,32},{32,36}... | collective-permute-start | bytes 3145736 | tf_op jit(solution)/shard_map/ppermute | solution.py:12
  59.8 30.4 %collective-permute-start.3 = (bf16[128,32,128]{2,0,1:T(8,128)(2,1)}, bf16[128,32,128]{2,0,1:T(8,128)(2,1)}, u32[]{:S(2)}, u32[]{:S(2)}) collective-permute-start(bf16[128,32,128]{2,0,1:T(8,128)(2,1)} %get-tuple-element.15), channel_id=1, source_target_pairs={{0,8},{4,12},{8,16},{12,20},{16,24},{20,28},{24,32},{28,36},{32,40... | collective-permute-start | bytes 3145736 | tf_op jit(solution)/shard_map/ppermute | solution.py:12
  101.5 23.9 %collective-permute-start.4 = (bf16[128,512]{1,0:T(8,128)(2,1)S(1)}, bf16[128,512]{1,0:T(8,128)(2,1)}, u32[]{:S(2)}, u32[]{:S(2)}) collective-permute-start(bf16[128,512]{1,0:T(8,128)(2,1)S(1)} %fusion.7), channel_id=1, source_target_pairs={{0,4},{4,8},{8,12},{12,16},{16,20},{20,24},{24,28},{28,32},{32,36}... | collective-permute-start | bytes 393224 | tf_op jit(solution)/shard_map/ppermute | solution.py:17
  125.4 20.2 %copy-start.1 = (bf16[1,1024,512]{2,1,0:T(8,128)(2,1)S(1)}, bf16[1,1024,512]{2,1,0:T(8,128)(2,1)}, u32[]{:S(2)}) copy-start(bf16[1,1024,512]{2,1,0:T(8,128)(2,1)} %all-gather.8.cloned.1.call-done) | copy-start | bytes 3145732
  128.0 6.7 %collective-permute-start.5 = (bf16[128,512]{1,0:T(8,128)(2,1)}, bf16[128,512]{1,0:T(8,128)(2,1)S(1)}, u32[]{:S(2)}, u32[]{:S(2)}) collective-permute-start(bf16[128,512]{1,0:T(8,128)(2,1)} %subtract_convert_fusion.5), channel_id=1, source_target_pairs={{0,4},{4,8},{8,12},{12,16},{16,20},{20,24},{24,28},{28,32},{32,36}... | collective-permute-start | bytes 393224 | tf_op jit(solution)/shard_map/ppermute | solution.py:17
  128.0 6.7 %collective-permute-start.6 = (bf16[128,512]{1,0:T(8,128)(2,1)}, bf16[128,512]{1,0:T(8,128)(2,1)}, u32[]{:S(2)}, u32[]{:S(2)}) collective-permute-start(bf16[128,512]{1,0:T(8,128)(2,1)} %subtract_convert_fusion.5), channel_id=1, source_target_pairs={{0,252},{4,0},{8,4},{12,8},{16,12},{20,16},{24,20},{28,24},{32,28}... | collective-permute-start | bytes 393224 | tf_op jit(solution)/shard_map/ppermute | solution.py:17
  137.3 8.2 %collective-permute-start.7 = (bf16[128,512]{1,0:T(8,128)(2,1)}, bf16[128,512]{1,0:T(8,128)(2,1)S(1)}, u32[]{:S(2)}, u32[]{:S(2)}) collective-permute-start(bf16[128,512]{1,0:T(8,128)(2,1)} %subtract_convert_fusion.4), channel_id=1, source_target_pairs={{0,8},{4,12},{8,16},{12,20},{16,24},{20,28},{24,32},{28,36},{32,40... | collective-permute-start | bytes 393224 | tf_op jit(solution)/shard_map/ppermute | solution.py:17
  137.3 8.2 %collective-permute-start.8 = (bf16[128,512]{1,0:T(8,128)(2,1)}, bf16[128,512]{1,0:T(8,128)(2,1)}, u32[]{:S(2)}, u32[]{:S(2)}) collective-permute-start(bf16[128,512]{1,0:T(8,128)(2,1)} %subtract_convert_fusion.4), channel_id=1, source_target_pairs={{0,248},{4,252},{8,0},{12,4},{16,8},{20,12},{24,16},{28,20},{32,24... | collective-permute-start | bytes 393224 | tf_op jit(solution)/shard_map/ppermute | solution.py:17
  147.8 7.1 %collective-permute-start.10 = (bf16[128,512]{1,0:T(8,128)(2,1)}, bf16[128,512]{1,0:T(8,128)(2,1)S(1)}, u32[]{:S(2)}, u32[]{:S(2)}) collective-permute-start(bf16[128,512]{1,0:T(8,128)(2,1)} %subtract_convert_fusion.3), channel_id=1, source_target_pairs={{0,240},{4,244},{8,248},{12,252},{16,0},{20,4},{24,8},{28,12},{32,... | collective-permute-start | bytes 393224 | tf_op jit(solution)/shard_map/ppermute | solution.py:17
  148.9 11.9 %collective-permute-start.9 = (bf16[128,512]{1,0:T(8,128)(2,1)}, bf16[128,512]{1,0:T(8,128)(2,1)}, u32[]{:S(2)}, u32[]{:S(2)}) collective-permute-start(bf16[128,512]{1,0:T(8,128)(2,1)} %subtract_convert_fusion.3), channel_id=1, source_target_pairs={{0,16},{4,20},{8,24},{12,28},{16,32},{20,36},{24,40},{28,44},{32,4... | collective-permute-start | bytes 393224 | tf_op jit(solution)/shard_map/ppermute | solution.py:17
  163.0 15.9 %collective-permute-start.11 = (bf16[128,512]{1,0:T(8,128)(2,1)}, bf16[128,512]{1,0:T(8,128)(2,1)S(1)}, u32[]{:S(2)}, u32[]{:S(2)}) collective-permute-start(bf16[128,512]{1,0:T(8,128)(2,1)} %subtract_convert_fusion.2), channel_id=1, source_target_pairs={{0,32},{4,36},{8,40},{12,44},{16,48},{20,52},{24,56},{28,60},{32,6... | collective-permute-start | bytes 393224 | tf_op jit(solution)/shard_map/ppermute | solution.py:17
  163.0 15.9 %collective-permute-start.12 = (bf16[128,512]{1,0:T(8,128)(2,1)}, bf16[128,512]{1,0:T(8,128)(2,1)}, u32[]{:S(2)}, u32[]{:S(2)}) collective-permute-start(bf16[128,512]{1,0:T(8,128)(2,1)} %subtract_convert_fusion.2), channel_id=1, source_target_pairs={{0,224},{4,228},{8,232},{12,236},{16,240},{20,244},{24,248},{28,25... | collective-permute-start | bytes 393224 | tf_op jit(solution)/shard_map/ppermute | solution.py:17
  181.1 11.1 %copy-start.3 = (f32[128,32,128]{2,0,1:T(8,128)S(1)}, f32[128,32,128]{2,0,1:T(8,128)}, u32[]{:S(2)}) copy-start(f32[128,32,128]{2,0,1:T(8,128)} %get-tuple-element.13) | copy-start | bytes 6291460
  181.1 5.2 %collective-permute-start.13 = (bf16[128,512]{1,0:T(8,128)(2,1)}, bf16[128,512]{1,0:T(8,128)(2,1)S(1)}, u32[]{:S(2)}, u32[]{:S(2)}) collective-permute-start(bf16[128,512]{1,0:T(8,128)(2,1)} %subtract_convert_fusion.1), channel_id=1, source_target_pairs={{0,64},{4,68},{8,72},{12,76},{16,80},{20,84},{24,88},{28,92},{32,9... | collective-permute-start | bytes 393224 | tf_op jit(solution)/shard_map/ppermute | solution.py:17
  182.7 6.5 %collective-permute-start.14 = (bf16[128,512]{1,0:T(8,128)(2,1)}, bf16[128,512]{1,0:T(8,128)(2,1)S(1)}, u32[]{:S(2)}, u32[]{:S(2)}) collective-permute-start(bf16[128,512]{1,0:T(8,128)(2,1)} %subtract_convert_fusion.1), channel_id=1, source_target_pairs={{0,192},{4,196},{8,200},{12,204},{16,208},{20,212},{24,216},{28,22... | collective-permute-start | bytes 393224 | tf_op jit(solution)/shard_map/ppermute | solution.py:17
  189.6 10.4 %copy-start.2 = (bf16[1,512,512]{2,1,0:T(8,128)(2,1)S(1)}, bf16[1,512,512]{2,1,0:T(8,128)(2,1)}, u32[]{:S(2)}) copy-start(bf16[1,512,512]{2,1,0:T(8,128)(2,1)} %all-gather.2) | copy-start | bytes 1572868
  191.0 8.6 %collective-permute-start.15 = (bf16[2,128,512]{2,1,0:T(8,128)(2,1)S(1)}, bf16[2,128,512]{2,1,0:T(8,128)(2,1)S(1)}, u32[]{:S(2)}, u32[]{:S(2)}) collective-permute-start(bf16[2,128,512]{2,1,0:T(8,128)(2,1)S(1)} %pad_maximum_fusion), channel_id=1, source_target_pairs={{0,128},{4,132},{8,136},{12,140},{16,144},{20,148},{24,152},{28,15... | collective-permute-start | bytes 786440 | tf_op jit(solution)/shard_map/ppermute | solution.py:17
  200.0 1.0 copy-start.5
Sparse Core Ops, SparseCore 0:
  9.8 57.4 all-gather.5
  69.1 29.3 all-gather.7
where the time goes:
time: 208 us
  waiting for transfers between devices  65.6 us (32%)
  starting transfers between devices  44 us (21%)
  other arithmetic  29.1 us (14%)
  matrix products  26.6 us (13%)
  blocking collectives  15.8 us (8%)
  between operations  14.2 us (7%)
  local copies, waits for them, and re-layouts  12.4 us (6%)
    ppermute x12, waiting for transfers between devices, passed_along_2(): lax.ppermute(value, axis, [(i, (i + by) % devices) for i in range(devices)])  37 us
    ppermute x12, starting transfers between devices, passed_along_2(): lax.ppermute(value, axis, [(i, (i + by) % devices) for i in range(devices)])  29.2 us
    ppermute x4, waiting for transfers between devices, passed_along(): lax.ppermute(value, axis, [(source, source + steps) for source in range(i...  27.9 us
    dot_general x10, matrix products, multiply(): jnp.dot(operand, gathered[which_op], preferred_element_type=jnp.float32)  17.8 us
    scatter-add x1, other arithmetic, on_device(): jax.ops.segment_sum(updates, segment_ids, num_segments=span_rows * blocks)  17.1 us
    all_gather x1, blocking collectives, on_device(): lax.all_gather(node_couple[0], 'rhs', axis=1, tiled=True)  15.8 us
    ppermute x4, starting transfers between devices, passed_along(): lax.ppermute(value, axis, [(source, source + steps) for source in range(i...  14.8 us
    dot_general x1, matrix products, on_device(): jnp.einsum('ncr,nkrs->nkcs', solved, leaf_couple, preferred_element_type=...  6.99 us
  transfers between devices with their start and end apart: 18, of which 11 were waited for; matrix products, arithmetic and copies ran while one was open for 26% of the time, Pallas kernels for 0%

commit v1 on v0

--- a/solution.py
+++ b/solution.py
@@ -50,7 +50,15 @@
     gathered = (
         lax.all_gather(lift_ops[0], "rhs", axis=1, tiled=True),
         lax.all_gather(node_mix[0], "rhs", axis=1, tiled=True),
-        lax.all_gather(node_couple[0], "rhs", axis=1, tiled=True),
+        jnp.concatenate(
+            lax.all_to_all(
+                jnp.stack(lax.axis_size("rhs") * [node_couple[0]]),
+                axis_name="rhs",
+                split_axis=0,
+                concat_axis=0,
+            ),
+            axis=1,
+        ),
     )
 
     def multiply(operand, which_op):

time: 208 us -> 202 us (0.971)
  blocking collectives: 15.8 us -> 0 us
  starting transfers between devices: 44 us -> 48.4 us
  local copies, waits for them, and re-layouts: 12.4 us -> 15 us
    all_gather x1 -> x0, blocking collectives: 15.8 us -> none  [on_device(): lax.all_gather(node_couple[0], 'rhs', axis=1, tiled=True)]
    ppermute x12, waiting for transfers between devices: 37 us -> 43 us  [passed_along_2(): lax.ppermute(value, axis, [(i, (i + by) % devices) for i in range(devices)])]
    ppermute x4, waiting for transfers between devices: 27.9 us -> 22.3 us  [passed_along(): lax.ppermute(value, axis, [(source, source + steps) for source in range(i...]
    all_to_all x0 -> x1, starting transfers between devices: none -> 4.44 us  [on_device(): lax.all_to_all(jnp.stack(lax.axis_size('rhs') * [node_couple[0]]), axis_n...]
  transfers between devices with their start and end apart: 18 -> 19, of which waited for: 11 -> 13; matrix products, arithmetic and copies ran while one was open for 26% -> 28% of each run, Pallas kernels for 0% -> 0%
where the time goes in v1:
time: 202 us; the launch traced here: 200 us
  waiting for transfers between devices  66 us (33%)
  starting transfers between devices  48.4 us (24%)
  other arithmetic  29.5 us (15%)
  matrix products  27.2 us (13%)
  local copies, waits for them, and re-layouts  15 us (7%)
  between operations  14.2 us (7%)
    ppermute x12, waiting for transfers between devices, passed_along_2(): lax.ppermute(value, axis, [(i, (i + by) % devices) for i in range(devices)])  43 us
    ppermute x12, starting transfers between devices, passed_along_2(): lax.ppermute(value, axis, [(i, (i + by) % devices) for i in range(devices)])  28.9 us
    ppermute x4, waiting for transfers between devices, passed_along(): lax.ppermute(value, axis, [(source, source + steps) for source in range(i...  22.3 us
    dot_general x10, matrix products, multiply(): jnp.dot(operand, gathered[which_op], preferred_element_type=jnp.float32)  18.3 us
    scatter-add x1, other arithmetic, on_device(): jax.ops.segment_sum(updates, segment_ids, num_segments=span_rows * blocks)  17.2 us
    ppermute x4, starting transfers between devices, passed_along(): lax.ppermute(value, axis, [(source, source + steps) for source in range(i...  14.9 us
    dot_general x1, matrix products, on_device(): jnp.einsum('ncr,nkrs->nkcs', solved, leaf_couple, preferred_element_type=...  7.1 us
    convert_element_type x1, other arithmetic, on_device(): skeleton_rhs.reshape(columns, blocks * block_width).astype(jnp.bfloat16)  6.86 us
  transfers between devices with their start and end apart: 19, of which 13 were waited for; matrix products, arithmetic and copies ran while one was open for 28% of the time, Pallas kernels for 0%

profile of v1, /device:TPU:6, one launch (start us, length us, event | category | flops | bytes accessed | tf_op | source)
XLA Modules:
  0.0 200.2 jit_solution(6736441206878227390)
XLA Ops:
  10.7 7.1 %fusion.27 = f32[8,128,9,128]{3,1,2,0:T(8,128)} fusion(bf16[8,9,384,128]{3,2,1,0:T(8,128)(2,1)} %param.10, bf16[8,128,384]{2,1,0:T(8,128)(2,1)S(1)} %convolution_convert_fusion), kind=kOutput, calls=%fused_computation.34 | convolution fusion | flops 905969664 | bytes 12582912 | tf_op jit(solution)/shard_map/ncr,nkrs->nkcs/dot_general | solution.py:32
  17.8 5.3 %broadcast_in_dim.10 = f32[160,128,128]{2,1,0:T(8,128)} broadcast(f32[]{:T(128)} %constant.30.clone.1), dimensions={} | broadcast | bytes 10485764 | tf_op jit(solution)/shard_map/broadcast_in_dim | solution.py:42
  23.1 17.2 %scatter_fusion = f32[160,128,128]{2,1,0:T(8,128)} fusion(f32[160,128,128]{2,1,0:T(8,128)} %broadcast_in_dim.10, s32[72]{0:T(128)S(1)} %fusion.67, f32[72,128,128]{2,1,0:T(8,128)} %bitcast.110), kind=kCustom, calls=%fused_computation | custom fusion | flops 1179648 | bytes 14156064 | tf_op jit(solution)/shard_map/scatter-add | solution.py:42
  40.3 5.4 %convert.6 = bf16[5,128,32,128]{3,1,2,0:T(8,128)(2,1)S(1)} convert(f32[5,128,32,128]{3,1,2,0:T(8,128)} %bitcast.101) | non-fusion elementwise | flops 2621440 | bytes 15728640 | tf_op jit(solution)/shard_map/convert.3
  47.8 7.9 %collective-permute-start = (bf16[128,32,128]{2,0,1:T(8,128)(2,1)}, bf16[128,32,128]{2,0,1:T(8,128)(2,1)}, u32[]{:S(2)}, u32[]{:S(2)}) collective-permute-start(bf16[128,32,128]{2,0,1:T(8,128)(2,1)} %get-tuple-element.14), channel_id=1, source_target_pairs={{8,0},{12,4},{16,8},{20,12},{24,16},{28,20},{32,24},{36,28},{40,32... | collective-permute-start | bytes 3145736 | tf_op jit(solution)/shard_map/ppermute | solution.py:12
  60.1 2.6 %collective-permute-start.3 = (bf16[128,32,128]{2,0,1:T(8,128)(2,1)}, bf16[128,32,128]{2,0,1:T(8,128)(2,1)}, u32[]{:S(2)}, u32[]{:S(2)}) collective-permute-start(bf16[128,32,128]{2,0,1:T(8,128)(2,1)} %get-tuple-element.15), channel_id=1, source_target_pairs={{0,8},{4,12},{8,16},{12,20},{16,24},{20,28},{24,32},{28,36},{32,40... | collective-permute-start | bytes 3145736 | tf_op jit(solution)/shard_map/ppermute | solution.py:12
  63.8 4.4 %all-to-all-start = ((bf16[4,512,128]{1,2,0:T(8,128)(2,1)}), bf16[4,512,128]{1,2,0:T(8,128)(2,1)S(1)}, u32[]{:S(2)}, u32[]{:S(2)}) async-start(bf16[4,512,128]{1,2,0:T(8,128)(2,1)} %stack.12), calls=%async_computation | async-start | bytes 1048576 | tf_op jit(solution)/shard_map/all_to_all | solution.py:54
  68.2 10.3 %collective-permute-done = bf16[128,32,128]{2,0,1:T(8,128)(2,1)} collective-permute-done((bf16[128,32,128]{2,0,1:T(8,128)(2,1)}, bf16[128,32,128]{2,0,1:T(8,128)(2,1)}, u32[]{:S(2)}, u32[]{:S(2)}) %collective-permute-start) | collective-permute-done | bytes 1048608 | tf_op jit(solution)/shard_map/ppermute | solution.py:12
  78.5 11.2 %collective-permute-done.1 = bf16[128,32,128]{2,0,1:T(8,128)(2,1)} collective-permute-done((bf16[128,32,128]{2,0,1:T(8,128)(2,1)}, bf16[128,32,128]{2,0,1:T(8,128)(2,1)}, u32[]{:S(2)}, u32[]{:S(2)}) %collective-permute-start.1) | collective-permute-done | bytes 1048608 | tf_op jit(solution)/shard_map/ppermute | solution.py:12
  90.5 6.9 %fusion.100 = (bf16[128,32,128]{2,0,1:T(8,128)(2,1)}, f32[128,32,128]{2,0,1:T(8,128)}) fusion(bf16[128,32,128]{2,0,1:T(8,128)(2,1)} %collective-permute-done.3, bf16[128,32,128]{2,0,1:T(8,128)(2,1)} %collective-permute-done.2, bf16[128,32,128]{2,0,1:T(8,128)(2,1)} %collective-permute-done.1, bf16[128,32,128]{2,0,1:T(8,128)(2,1)} %collective-permute-done, ...), kind=kLoop, calls=%fused_computation.82 | loop fusion | flops 5242880 | bytes 11534336 | tf_op jit(solution)/shard_map/convert_element_type | solution.py:75
  99.6 3.3 %fusion.7 = bf16[128,512]{1,0:T(8,128)(2,1)S(1)} fusion(bf16[128,4096]{0,1:T(8,128)(2,1)} %bitcast.111, bf16[1,4096,512]{2,1,0:T(8,128)(2,1)} %all-gather.5.cloned.1.call-done), kind=kOutput, calls=%fused_computation.10 | convolution fusion | flops 536936448 | bytes 5373952 | tf_op jit(solution)/shard_map/dot_general | solution.py:65
  102.9 8.2 %collective-permute-start.4 = (bf16[128,512]{1,0:T(8,128)(2,1)S(1)}, bf16[128,512]{1,0:T(8,128)(2,1)}, u32[]{:S(2)}, u32[]{:S(2)}) collective-permute-start(bf16[128,512]{1,0:T(8,128)(2,1)S(1)} %fusion.7), channel_id=1, source_target_pairs={{0,4},{4,8},{8,12},{12,16},{16,20},{20,24},{24,28},{28,32},{32,36}... | collective-permute-start | bytes 393224 | tf_op jit(solution)/shard_map/ppermute | solution.py:17
  113.3 2.6 %subtract_convert_fusion.5 = bf16[128,512]{1,0:T(8,128)(2,1)} fusion(bf16[128,512]{1,0:T(8,128)(2,1)S(1)} %fusion.7, bf16[128,512]{1,0:T(8,128)(2,1)} %collective-permute-done.4, bf16[512,512]{0,1:T(8,128)(2,1)} %bitcast.103, bf16[1,1024,512]{2,1,0:T(8,128)(2,1)} %all-gather.7.cloned.1.call-done), kind=kOutput, calls=%fused_computation.64 | convolution fusion | flops 202309632 | bytes 1966080 | tf_op jit(solution)/shard_map/dot_general | solution.py:65
  115.9 3.9 %collective-permute-start.6 = (bf16[128,512]{1,0:T(8,128)(2,1)}, bf16[128,512]{1,0:T(8,128)(2,1)}, u32[]{:S(2)}, u32[]{:S(2)}) collective-permute-start(bf16[128,512]{1,0:T(8,128)(2,1)} %subtract_convert_fusion.5), channel_id=1, source_target_pairs={{0,252},{4,0},{8,4},{12,8},{16,12},{20,16},{24,20},{28,24},{32,28}... | collective-permute-start | bytes 393224 | tf_op jit(solution)/shard_map/ppermute | solution.py:17
  119.7 2.9 %collective-permute-done.5 = bf16[128,512]{1,0:T(8,128)(2,1)S(1)} collective-permute-done((bf16[128,512]{1,0:T(8,128)(2,1)}, bf16[128,512]{1,0:T(8,128)(2,1)S(1)}, u32[]{:S(2)}, u32[]{:S(2)}) %collective-permute-start.5) | collective-permute-done | bytes 131104 | tf_op jit(solution)/shard_map/ppermute | solution.py:17
  125.3 4.1 %collective-permute-start.8 = (bf16[128,512]{1,0:T(8,128)(2,1)}, bf16[128,512]{1,0:T(8,128)(2,1)}, u32[]{:S(2)}, u32[]{:S(2)}) collective-permute-start(bf16[128,512]{1,0:T(8,128)(2,1)} %subtract_convert_fusion.4), channel_id=1, source_target_pairs={{0,248},{4,252},{8,0},{12,4},{16,8},{20,12},{24,16},{28,20},{32,24... | collective-permute-start | bytes 393224 | tf_op jit(solution)/shard_map/ppermute | solution.py:17
  129.3 4.1 %collective-permute-done.7 = bf16[128,512]{1,0:T(8,128)(2,1)S(1)} collective-permute-done((bf16[128,512]{1,0:T(8,128)(2,1)}, bf16[128,512]{1,0:T(8,128)(2,1)S(1)}, u32[]{:S(2)}, u32[]{:S(2)}) %collective-permute-start.7) | collective-permute-done | bytes 131104 | tf_op jit(solution)/shard_map/ppermute | solution.py:17
  138.6 5.5 %collective-permute-done.10 = bf16[128,512]{1,0:T(8,128)(2,1)S(1)} collective-permute-done((bf16[128,512]{1,0:T(8,128)(2,1)}, bf16[128,512]{1,0:T(8,128)(2,1)S(1)}, u32[]{:S(2)}, u32[]{:S(2)}) %collective-permute-start.10) | collective-permute-done | bytes 131104 | tf_op jit(solution)/shard_map/ppermute | solution.py:17
  144.1 4.6 %collective-permute-done.9 = bf16[128,512]{1,0:T(8,128)(2,1)} collective-permute-done((bf16[128,512]{1,0:T(8,128)(2,1)}, bf16[128,512]{1,0:T(8,128)(2,1)}, u32[]{:S(2)}, u32[]{:S(2)}) %collective-permute-start.9) | collective-permute-done | bytes 131104 | tf_op jit(solution)/shard_map/ppermute | solution.py:17
  151.0 6.8 %collective-permute-start.12 = (bf16[128,512]{1,0:T(8,128)(2,1)}, bf16[128,512]{1,0:T(8,128)(2,1)}, u32[]{:S(2)}, u32[]{:S(2)}) collective-permute-start(bf16[128,512]{1,0:T(8,128)(2,1)} %subtract_convert_fusion.2), channel_id=1, source_target_pairs={{0,224},{4,228},{8,232},{12,236},{16,240},{20,244},{24,248},{28,25... | collective-permute-start | bytes 393224 | tf_op jit(solution)/shard_map/ppermute | solution.py:17
  157.8 7.7 %collective-permute-done.11 = bf16[128,512]{1,0:T(8,128)(2,1)S(1)} collective-permute-done((bf16[128,512]{1,0:T(8,128)(2,1)}, bf16[128,512]{1,0:T(8,128)(2,1)S(1)}, u32[]{:S(2)}, u32[]{:S(2)}) %collective-permute-start.11) | collective-permute-done | bytes 131104 | tf_op jit(solution)/shard_map/ppermute | solution.py:17
  165.5 6.6 %collective-permute-done.12 = bf16[128,512]{1,0:T(8,128)(2,1)} collective-permute-done((bf16[128,512]{1,0:T(8,128)(2,1)}, bf16[128,512]{1,0:T(8,128)(2,1)}, u32[]{:S(2)}, u32[]{:S(2)}) %collective-permute-start.12) | collective-permute-done | bytes 131104 | tf_op jit(solution)/shard_map/ppermute | solution.py:17
  176.4 3.6 %collective-permute-done.13 = bf16[128,512]{1,0:T(8,128)(2,1)S(1)} collective-permute-done((bf16[128,512]{1,0:T(8,128)(2,1)}, bf16[128,512]{1,0:T(8,128)(2,1)S(1)}, u32[]{:S(2)}, u32[]{:S(2)}) %collective-permute-start.13) | collective-permute-done | bytes 131104 | tf_op jit(solution)/shard_map/ppermute | solution.py:17
  186.5 5.5 %collective-permute-done.15 = bf16[2,128,512]{2,1,0:T(8,128)(2,1)S(1)} collective-permute-done((bf16[2,128,512]{2,1,0:T(8,128)(2,1)S(1)}, bf16[2,128,512]{2,1,0:T(8,128)(2,1)S(1)}, u32[]{:S(2)}, u32[]{:S(2)}) %collective-permute-start.15) | collective-permute-done | bytes 262176 | tf_op jit(solution)/shard_map/ppermute | solution.py:17
  (57 shorter events, 38.4 us)
Async XLA Ops:
  7.2 92.5 %all-gather.5.cloned.1.call-start = ((), (), s32[]{:S(2)}) async-start(), calls=%async_computation.1 | async-start | bytes 5242880 | tf_op jit(solution)/shard_map/all_gather | solution.py:51
  7.9 104.0 %all-gather.7.cloned.1.call-start = ((), (), s32[]{:S(2)}) async-start(), calls=%async_computation.2 | async-start | bytes 1310720 | tf_op jit(solution)/shard_map/all_gather | solution.py:52
  10.7 7.1 %copy-start.5 = (bf16[8,128,384]{2,1,0:T(8,128)(2,1)}, bf16[8,128,384]{2,1,0:T(8,128)(2,1)S(1)}, u32[]{:S(2)}) copy-start(bf16[8,128,384]{2,1,0:T(8,128)(2,1)S(1)} %convolution_convert_fusion) | copy-start | bytes 2359300
  45.7 17.1 %copy-start.7 = (bf16[1,512,128]{2,1,0:T(8,128)(2,1)S(1)}, bf16[1,512,128]{2,1,0:T(8,128)(2,1)}, u32[]{:S(2)}) copy-start(bf16[1,512,128]{2,1,0:T(8,128)(2,1)} %param.15) | copy-start | bytes 393220
  47.8 30.7 %collective-permute-start = (bf16[128,32,128]{2,0,1:T(8,128)(2,1)}, bf16[128,32,128]{2,0,1:T(8,128)(2,1)}, u32[]{:S(2)}, u32[]{:S(2)}) collective-permute-start(bf16[128,32,128]{2,0,1:T(8,128)(2,1)} %get-tuple-element.14), channel_id=1, source_target_pairs={{8,0},{12,4},{16,8},{20,12},{24,16},{28,20},{32,24},{36,28},{40,32... | collective-permute-start | bytes 3145736 | tf_op jit(solution)/shard_map/ppermute | solution.py:12
  55.7 34.0 %collective-permute-start.1 = (bf16[128,32,128]{2,0,1:T(8,128)(2,1)}, bf16[128,32,128]{2,0,1:T(8,128)(2,1)}, u32[]{:S(2)}, u32[]{:S(2)}) collective-permute-start(bf16[128,32,128]{2,0,1:T(8,128)(2,1)} %get-tuple-element.17), channel_id=1, source_target_pairs={{4,0},{8,4},{12,8},{16,12},{20,16},{24,20},{28,24},{32,28},{36,32}... | collective-permute-start | bytes 3145736 | tf_op jit(solution)/shard_map/ppermute | solution.py:12
  57.8 32.0 %collective-permute-start.2 = (bf16[128,32,128]{2,0,1:T(8,128)(2,1)}, bf16[128,32,128]{2,0,1:T(8,128)(2,1)}, u32[]{:S(2)}, u32[]{:S(2)}) collective-permute-start(bf16[128,32,128]{2,0,1:T(8,128)(2,1)} %get-tuple-element.16), channel_id=1, source_target_pairs={{0,4},{4,8},{8,12},{12,16},{16,20},{20,24},{24,28},{28,32},{32,36}... | collective-permute-start | bytes 3145736 | tf_op jit(solution)/shard_map/ppermute | solution.py:12
  60.1 30.4 %collective-permute-start.3 = (bf16[128,32,128]{2,0,1:T(8,128)(2,1)}, bf16[128,32,128]{2,0,1:T(8,128)(2,1)}, u32[]{:S(2)}, u32[]{:S(2)}) collective-permute-start(bf16[128,32,128]{2,0,1:T(8,128)(2,1)} %get-tuple-element.15), channel_id=1, source_target_pairs={{0,8},{4,12},{8,16},{12,20},{16,24},{20,28},{24,32},{28,36},{32,40... | collective-permute-start | bytes 3145736 | tf_op jit(solution)/shard_map/ppermute | solution.py:12
  63.8 47.3 %all-to-all-start = ((bf16[4,512,128]{1,2,0:T(8,128)(2,1)}), bf16[4,512,128]{1,2,0:T(8,128)(2,1)S(1)}, u32[]{:S(2)}, u32[]{:S(2)}) async-start(bf16[4,512,128]{1,2,0:T(8,128)(2,1)} %stack.12), calls=%async_computation | async-start | bytes 1048576 | tf_op jit(solution)/shard_map/all_to_all | solution.py:54
  102.9 10.4 %collective-permute-start.4 = (bf16[128,512]{1,0:T(8,128)(2,1)S(1)}, bf16[128,512]{1,0:T(8,128)(2,1)}, u32[]{:S(2)}, u32[]{:S(2)}) collective-permute-start(bf16[128,512]{1,0:T(8,128)(2,1)S(1)} %fusion.7), channel_id=1, source_target_pairs={{0,4},{4,8},{8,12},{12,16},{16,20},{20,24},{24,28},{28,32},{32,36}... | collective-permute-start | bytes 393224 | tf_op jit(solution)/shard_map/ppermute | solution.py:17
  111.9 21.5 %copy-start.1 = (bf16[1,1024,512]{2,1,0:T(8,128)(2,1)S(1)}, bf16[1,1024,512]{2,1,0:T(8,128)(2,1)}, u32[]{:S(2)}) copy-start(bf16[1,1024,512]{2,1,0:T(8,128)(2,1)} %all-gather.7.cloned.1.call-done) | copy-start | bytes 3145732
  115.9 6.7 %collective-permute-start.5 = (bf16[128,512]{1,0:T(8,128)(2,1)}, bf16[128,512]{1,0:T(8,128)(2,1)S(1)}, u32[]{:S(2)}, u32[]{:S(2)}) collective-permute-start(bf16[128,512]{1,0:T(8,128)(2,1)} %subtract_convert_fusion.5), channel_id=1, source_target_pairs={{0,4},{4,8},{8,12},{12,16},{16,20},{20,24},{24,28},{28,32},{32,36}... | collective-permute-start | bytes 393224 | tf_op jit(solution)/shard_map/ppermute | solution.py:17
  115.9 6.7 %collective-permute-start.6 = (bf16[128,512]{1,0:T(8,128)(2,1)}, bf16[128,512]{1,0:T(8,128)(2,1)}, u32[]{:S(2)}, u32[]{:S(2)}) collective-permute-start(bf16[128,512]{1,0:T(8,128)(2,1)} %subtract_convert_fusion.5), channel_id=1, source_target_pairs={{0,252},{4,0},{8,4},{12,8},{16,12},{20,16},{24,20},{28,24},{32,28}... | collective-permute-start | bytes 393224 | tf_op jit(solution)/shard_map/ppermute | solution.py:17
  125.2 8.2 %collective-permute-start.7 = (bf16[128,512]{1,0:T(8,128)(2,1)}, bf16[128,512]{1,0:T(8,128)(2,1)S(1)}, u32[]{:S(2)}, u32[]{:S(2)}) collective-permute-start(bf16[128,512]{1,0:T(8,128)(2,1)} %subtract_convert_fusion.4), channel_id=1, source_target_pairs={{0,8},{4,12},{8,16},{12,20},{16,24},{20,28},{24,32},{28,36},{32,40... | collective-permute-start | bytes 393224 | tf_op jit(solution)/shard_map/ppermute | solution.py:17
  125.3 8.2 %collective-permute-start.8 = (bf16[128,512]{1,0:T(8,128)(2,1)}, bf16[128,512]{1,0:T(8,128)(2,1)}, u32[]{:S(2)}, u32[]{:S(2)}) collective-permute-start(bf16[128,512]{1,0:T(8,128)(2,1)} %subtract_convert_fusion.4), channel_id=1, source_target_pairs={{0,248},{4,252},{8,0},{12,4},{16,8},{20,12},{24,16},{28,20},{32,24... | collective-permute-start | bytes 393224 | tf_op jit(solution)/shard_map/ppermute | solution.py:17
  135.7 8.4 %collective-permute-start.10 = (bf16[128,512]{1,0:T(8,128)(2,1)}, bf16[128,512]{1,0:T(8,128)(2,1)S(1)}, u32[]{:S(2)}, u32[]{:S(2)}) collective-permute-start(bf16[128,512]{1,0:T(8,128)(2,1)} %subtract_convert_fusion.3), channel_id=1, source_target_pairs={{0,240},{4,244},{8,248},{12,252},{16,0},{20,4},{24,8},{28,12},{32,... | collective-permute-start | bytes 393224 | tf_op jit(solution)/shard_map/ppermute | solution.py:17
  136.8 11.9 %collective-permute-start.9 = (bf16[128,512]{1,0:T(8,128)(2,1)}, bf16[128,512]{1,0:T(8,128)(2,1)}, u32[]{:S(2)}, u32[]{:S(2)}) collective-permute-start(bf16[128,512]{1,0:T(8,128)(2,1)} %subtract_convert_fusion.3), channel_id=1, source_target_pairs={{0,16},{4,20},{8,24},{12,28},{16,32},{20,36},{24,40},{28,44},{32,4... | collective-permute-start | bytes 393224 | tf_op jit(solution)/shard_map/ppermute | solution.py:17
  151.0 14.5 %collective-permute-start.11 = (bf16[128,512]{1,0:T(8,128)(2,1)}, bf16[128,512]{1,0:T(8,128)(2,1)S(1)}, u32[]{:S(2)}, u32[]{:S(2)}) collective-permute-start(bf16[128,512]{1,0:T(8,128)(2,1)} %subtract_convert_fusion.2), channel_id=1, source_target_pairs={{0,32},{4,36},{8,40},{12,44},{16,48},{20,52},{24,56},{28,60},{32,6... | collective-permute-start | bytes 393224 | tf_op jit(solution)/shard_map/ppermute | solution.py:17
  151.0 21.1 %collective-permute-start.12 = (bf16[128,512]{1,0:T(8,128)(2,1)}, bf16[128,512]{1,0:T(8,128)(2,1)}, u32[]{:S(2)}, u32[]{:S(2)}) collective-permute-start(bf16[128,512]{1,0:T(8,128)(2,1)} %subtract_convert_fusion.2), channel_id=1, source_target_pairs={{0,224},{4,228},{8,232},{12,236},{16,240},{20,244},{24,248},{28,25... | collective-permute-start | bytes 393224 | tf_op jit(solution)/shard_map/ppermute | solution.py:17
  174.4 9.6 %copy-start.4 = (f32[128,32,128]{2,0,1:T(8,128)S(1)}, f32[128,32,128]{2,0,1:T(8,128)}, u32[]{:S(2)}) copy-start(f32[128,32,128]{2,0,1:T(8,128)} %get-tuple-element.13) | copy-start | bytes 6291460
  174.4 5.6 %collective-permute-start.13 = (bf16[128,512]{1,0:T(8,128)(2,1)}, bf16[128,512]{1,0:T(8,128)(2,1)S(1)}, u32[]{:S(2)}, u32[]{:S(2)}) collective-permute-start(bf16[128,512]{1,0:T(8,128)(2,1)} %subtract_convert_fusion.1), channel_id=1, source_target_pairs={{0,64},{4,68},{8,72},{12,76},{16,80},{20,84},{24,88},{28,92},{32,9... | collective-permute-start | bytes 393224 | tf_op jit(solution)/shard_map/ppermute | solution.py:17
  174.4 6.8 %collective-permute-start.14 = (bf16[128,512]{1,0:T(8,128)(2,1)}, bf16[128,512]{1,0:T(8,128)(2,1)S(1)}, u32[]{:S(2)}, u32[]{:S(2)}) collective-permute-start(bf16[128,512]{1,0:T(8,128)(2,1)} %subtract_convert_fusion.1), channel_id=1, source_target_pairs={{0,192},{4,196},{8,200},{12,204},{16,208},{20,212},{24,216},{28,22... | collective-permute-start | bytes 393224 | tf_op jit(solution)/shard_map/ppermute | solution.py:17
  181.6 10.8 %copy-start.3 = (bf16[4,512,128]{1,2,0:T(8,128)(2,1)S(1)}, bf16[4,512,128]{1,2,0:T(8,128)(2,1)}, u32[]{:S(2)}) copy-start(bf16[4,512,128]{1,2,0:T(8,128)(2,1)} %copy-done.2) | copy-start | bytes 1572868
  183.0 9.0 %collective-permute-start.15 = (bf16[2,128,512]{2,1,0:T(8,128)(2,1)S(1)}, bf16[2,128,512]{2,1,0:T(8,128)(2,1)S(1)}, u32[]{:S(2)}, u32[]{:S(2)}) collective-permute-start(bf16[2,128,512]{2,1,0:T(8,128)(2,1)S(1)} %pad_maximum_fusion), channel_id=1, source_target_pairs={{0,128},{4,132},{8,136},{12,140},{16,144},{20,148},{24,152},{28,15... | collective-permute-start | bytes 786440 | tf_op jit(solution)/shard_map/ppermute | solution.py:17
  (3 other events, 3.5 us)
Sparse Core Ops, SparseCore 0:
  9.8 57.4 all-gather.4
  69.1 29.3 all-gather.6
